TPU v7x, 32 devices: a whole 2x2x4 slice. The times are simulated.
32 devices in a mesh: row: 4 (over y, core), col: 8 (over z, x).
Axes of the slice: x: 2, y: 2, z: 4, core: 2. Of those that a mesh axis runs over, the one named last changes fastest.
Arguments:
- contribution: float32 [8, 4, 4, 8, 128, 128], P(None, 'row', None, 'col'), may hold values from -6 to 6
- parent_tiles: float32 [16, 4, 8, 8, 128, 128], P(None, 'row', None, 'col'), may hold values from -6 to 6
- row_basis: float32 [8, 4, 64, 128], P(None, 'row'), may hold values from -2.4 to 2.4
- pivot_basis: float32 [8, 4, 64, 2048], P(None, 'row', None, 'col'), may hold values from -0.125 to 0.125
- tile_ranks: int32 [32], replicated, may hold values from 16 to 64, as said below
- block_map: int32 [32], replicated, may hold values from 0 to 63, as said below
- panel_start: int32 [1], replicated, may hold values from 0 to 31
- pivot_inverse: float32 [512, 512], replicated
Outputs:
- updated_parent: float32 [16, 4, 8, 8, 128, 128], P(None, 'row', None, 'col')
Inputs may be any that keep to these rules, and one draw needn't show every extreme that they name: `tile_ranks`: multiples of 16; both 16 and 64 occur. `block_map`: child tile row u * 8 + l, for 0 <= l < 8, maps to parent tile row 2 * 8 * u + h_u + l with 0 <= h_u < 8; the 4 values h_u are distinct modulo 4.
All inputs are finite; a program needn't handle non-finite values.
Results may differ from a plain program's by a relative error of at most 0.0003.
Values sent between devices are 32-bit elements; how exact they have to be, the bound alone decides.
A program may use at most 128 MiB of HBM per device.

v0:
```python
import jax
import jax.numpy as jnp
from jax import lax
from jax.sharding import PartitionSpec as P

PANEL_T = 4
highest = lax.Precision.HIGHEST


def spread_2(x, axis, root):
    mine = lax.axis_index(axis) == root
    return lax.psum(jnp.where(mine, x, jnp.zeros_like(x)), axis)


def select_entries(lookup, wanted):
    matches = wanted[:, None] == jnp.arange(lookup.shape[0], dtype=jnp.int32)[None, :]
    return jnp.sum(jnp.where(matches, lookup[None, :], 0), axis=1)


def keep_ranks(factor, tile_index, rank_table):
    limits = select_entries(rank_table, tile_index)
    kept_cols = (jnp.arange(factor.shape[1], dtype=jnp.int32)[None, :] < limits[:, None]).astype(
        jnp.float32
    )
    return factor * kept_cols[:, :, None]


def every_other(stacked, groups, offset):
    shaped = stacked.reshape((groups, stacked.shape[0] // groups) + stacked.shape[1:])
    return lax.dynamic_index_in_dim(shaped, offset, axis=1, keepdims=False)


def per_device(
    contribution,
    parent_tiles,
    row_basis,
    pivot_basis,
    tile_ranks,
    block_map,
    panel_start,
    pivot_inverse,
):
    rows_grid = lax.axis_size("row")
    cols_grid = lax.axis_size("col")
    my_row = lax.axis_index("row")
    my_col = lax.axis_index("col")
    local_rows = contribution.shape[0]
    local_cols = contribution.shape[2]
    parent_rows = parent_tiles.shape[0]
    parent_cols = parent_tiles.shape[2]
    rank_max = row_basis.shape[2]
    per_block = cols_grid // rows_grid
    row_index = jnp.arange(local_rows, dtype=jnp.int32) * rows_grid + my_row
    col_index = jnp.arange(local_cols, dtype=jnp.int32) * cols_grid + my_col
    root_row = my_col % rows_grid
    offset = my_col // rows_grid
    own_basis = keep_ranks(row_basis[:, 0], row_index, tile_ranks)
    own_pivots = pivot_basis[:, 0]
    basis_picked = every_other(row_basis[:, 0], local_cols, offset)
    col_basis = spread_2(basis_picked, "row", root_row)
    all_pivots = lax.all_gather(pivot_basis, "row", axis=1, tiled=True)
    pivot_width = pivot_basis.shape[3]
    grouped = all_pivots.reshape(local_cols, cols_grid, rank_max, pivot_width)
    products = jnp.einsum(
        "trp,scup->cstru",
        own_pivots,
        grouped,
        precision=highest,
        preferred_element_type=jnp.float32,
    )
    weights = lax.psum_scatter(
        products.reshape(lax.axis_size("col") * local_cols, local_rows, rank_max * rank_max),
        "col",
        scatter_dimension=0,
        tiled=True,
    )
    weights = weights.reshape(local_cols, local_rows, rank_max, rank_max)
    col_basis = keep_ranks(col_basis, col_index, tile_ranks)
    half_product = jnp.einsum(
        "trx,stru->tsux", own_basis, weights, precision=highest, preferred_element_type=jnp.float32
    )
    update = jnp.einsum(
        "tsux,suy->tsxy",
        half_product,
        col_basis,
        precision=highest,
        preferred_element_type=jnp.float32,
    )
    lower_mask = (row_index[:, None] >= col_index[None, :])[:, :, None, None]
    payload = jnp.where(lower_mask, contribution[:, 0, :, 0] - update, jnp.float32(0.0))
    block_first = jnp.arange(local_cols, dtype=jnp.int32) * cols_grid
    shifts = select_entries(block_map, block_first) - 2 * block_first
    row_shift = jnp.repeat(shifts, per_block) % rows_grid
    positions = jnp.arange(local_rows, dtype=jnp.int32)
    grid_rows = jnp.arange(rows_grid, dtype=jnp.int32)
    block_rows = jnp.arange(per_block, dtype=jnp.int32)
    target = (my_row + row_shift) % rows_grid
    buckets = (target[None, None, :] == grid_rows[:, None, None]) & (
        positions[None, None, :] % per_block == block_rows[None, :, None]
    )
    packed = jnp.einsum(
        "rlt,tsxy->rlsxy",
        buckets.astype(jnp.float32),
        payload,
        precision=highest,
        preferred_element_type=jnp.float32,
    )
    arrived = lax.all_to_all(packed, "row", split_axis=0, concat_axis=0, tiled=True)
    source = (my_row - row_shift) % rows_grid
    chosen = (source[:, None, None] == grid_rows[None, :, None]) & (
        positions[:, None, None] % per_block == block_rows[None, None, :]
    )
    payload = jnp.einsum(
        "tpl,plsxy->tsxy",
        chosen.astype(jnp.float32),
        arrived,
        precision=highest,
        preferred_element_type=jnp.float32,
    )
    grid_cols = jnp.arange(cols_grid, dtype=jnp.int32)
    target = (my_col + shifts) % cols_grid
    buckets = (grid_cols[:, None] == target[None, :]).astype(jnp.float32)
    packed = jnp.einsum(
        "cs,tsxy->ctxy", buckets, payload, precision=highest, preferred_element_type=jnp.float32
    )
    arrived = lax.all_to_all(packed, "col", split_axis=0, concat_axis=0, tiled=True)
    source = (my_col - shifts) % cols_grid
    chosen = (source[:, None] == grid_cols[None, :]).astype(jnp.float32)
    payload = jnp.einsum(
        "sq,qtxy->tsxy", chosen, arrived, precision=highest, preferred_element_type=jnp.float32
    )
    row_source = (my_row - row_shift) % rows_grid
    target_rows = (
        select_entries(block_map, jnp.arange(local_rows, dtype=jnp.int32) * rows_grid + row_source)
        // rows_grid
    )
    col_source = (my_col - shifts) % cols_grid
    target_cols = (
        select_entries(block_map, jnp.arange(local_cols, dtype=jnp.int32) * cols_grid + col_source)
        // cols_grid
    )
    row_place = (jnp.arange(parent_rows, dtype=jnp.int32)[:, None] == target_rows[None, :]).astype(
        jnp.float32
    )
    col_place = (jnp.arange(parent_cols, dtype=jnp.int32)[:, None] == target_cols[None, :]).astype(
        jnp.float32
    )
    spread = jnp.einsum(
        "at,tsxy->asxy", row_place, payload, precision=highest, preferred_element_type=jnp.float32
    )
    spread = jnp.einsum(
        "bs,asxy->abxy", col_place, spread, precision=highest, preferred_element_type=jnp.float32
    )
    assembled = parent_tiles[:, 0, :, 0] + spread
    start_col = panel_start[0]
    panel_parts = []
    for panel_index in range(PANEL_T):
        column_id = start_col + panel_index
        column = lax.dynamic_index_in_dim(assembled, column_id // cols_grid, axis=1, keepdims=False)
        panel_parts.append(spread_2(column, "col", column_id % cols_grid))
    row_panel = jnp.concatenate(panel_parts, axis=2)
    col_panel = spread_2(every_other(row_panel, parent_cols, offset), "row", root_row)
    scaled = jnp.einsum(
        "axp,pq->axq",
        row_panel,
        pivot_inverse,
        precision=highest,
        preferred_element_type=jnp.float32,
    )
    trailing = jnp.einsum(
        "axq,byq->abxy", scaled, col_panel, precision=highest, preferred_element_type=jnp.float32
    )
    big_rows = jnp.arange(parent_rows, dtype=jnp.int32) * rows_grid + my_row
    big_cols = jnp.arange(parent_cols, dtype=jnp.int32) * cols_grid + my_col
    window = (big_rows[:, None] >= big_cols[None, :]) & (big_cols[None, :] >= start_col + PANEL_T)
    result = jnp.where(window[:, :, None, None], assembled - trailing, assembled)
    return result[:, None, :, None]


def solution(mesh):
    placed = (
        P(None, "row", None, "col", None, None),
        P(None, "row", None, "col", None, None),
        P(None, "row", None, None),
        P(None, "row", None, "col"),
        P(),
        P(),
        P(),
        P(),
    )
    return jax.shard_map(
        per_device,
        mesh=mesh,
        in_specs=placed,
        out_specs=P(None, "row", None, "col", None, None),
        check_vma=False,
    )
```

profile of v0, /device:TPU:0, one launch (start us, length us, event | category | flops | bytes accessed | tf_op | source)
XLA Modules:
  0.0 630.5 jit_solution(7358268247508881916)
XLA Ops:
  7.3 26.9 %all-gather.2.cloned.1.call-done = f32[8,4,64,256]{3,2,1,0:T(8,128)} async-done(((f32[8,1,64,256]{3,2,1,0:T(8,128)}), f32[8,4,64,256]{3,2,1,0:T(8,128)}) %all-gather.2.cloned.1.call-update) | async-done | bytes 2097168 | tf_op jit(solution)/shard_map/all_gather | solution.py:61
  34.2 10.3 %convolution_bitcast_fusion = f32[8,4,8,64,64]{3,4,2,0,1:T(8,128)} fusion(f32[4,8,64,256,1]{3,2,4,1,0:T(8,128)} %bitcast.130, f32[8,1,64,256]{3,2,1,0:T(8,128)} %param.11), kind=kOutput, calls=%fused_computation.9 | convolution fusion | flops 3221225472 | bytes 6815744 | tf_op jit(solution)/shard_map/trp,scup->cstru/dot_general | solution.py:64
  44.5 9.2 %copy.46 = f32[8,4,8,64,64]{4,3,2,1,0:T(8,128)} copy(f32[8,4,8,64,64]{3,4,2,0,1:T(8,128)} %convolution_bitcast_fusion) | data formatting | bytes 8388608 | tf_op jit(solution)/shard_map/trp,scup->cstru/transpose | solution.py:64
  53.7 7.9 %reshape.481 = f32[32,8,4096]{2,1,0:T(8,128)} reshape(f32[8,4,8,64,64]{4,3,2,1,0:T(8,128)} %copy.46) | data formatting | bytes 8388608 | tf_op jit(solution)/shard_map/reshape | solution.py:72
  66.2 83.9 %reduce-scatter.2.cloned.1.call-done = f32[4,8,4096]{2,1,0:T(8,128)} async-done(((f32[32,8,4096]{2,1,0:T(8,128)}), f32[4,8,4096]{2,1,0:T(8,128)}) %reduce-scatter.2.cloned.1.call-update) | async-done | bytes 524304 | tf_op jit(solution)/shard_map/reduce_scatter | solution.py:71
  152.5 4.1 fusion.28
  156.6 27.2 %all-reduce.5.cloned.1.call-done = f32[4,64,128]{2,1,0:T(8,128)} async-done(((f32[4,64,128]{2,1,0:T(8,128)}), f32[4,64,128]{2,1,0:T(8,128)}) %all-reduce.5.cloned.1.call-update) | async-done | bytes 131088 | tf_op jit(solution)/shard_map/psum | solution.py:12
  183.8 4.6 fusion.13
  190.5 4.0 fusion.11
  194.5 3.8 all-to-all-start
  198.3 25.6 %all-to-all-done = f32[4,2,4,128,128]{4,1,3,2,0:T(2,128)S(1)} async-done(((f32[4,2,4,128,128]{4,1,3,2,0:T(2,128)}), f32[4,2,4,128,128]{4,1,3,2,0:T(2,128)S(1)}, u32[]{:S(2)}, u32[]{:S(2)}) %all-to-all-start) | async-done | bytes 2097184 | tf_op jit(solution)/shard_map/all_to_all | solution.py:108
  227.2 3.6 fusion.16
  233.6 5.5 all-to-all-start.1
  240.5 91.6 %all-to-all-done.1 = f32[8,8,128,128]{3,2,1,0:T(8,128)} async-done(((f32[8,8,128,128]{3,2,1,0:T(8,128)}), f32[8,8,128,128]{3,2,1,0:T(8,128)}, u32[]{:S(2)}, u32[]{:S(2)}) %all-to-all-start.1) | async-done | bytes 4194336 | tf_op jit(solution)/shard_map/all_to_all | solution.py:126
  332.1 6.4 %fusion.23 = f32[8,4,128,128]{3,1,2,0:T(4,128)S(1)} fusion(f32[8,8,128,128]{3,2,1,0:T(8,128)} %all-to-all-done.1, s32[4]{0:T(128)S(1)} %get-tuple-element.10), kind=kOutput, calls=%fused_computation.25 | convolution fusion | flops 50331680 | bytes 6291472 | tf_op jit(solution)/shard_map/sq,qtxy->tsxy/dot_general | solution.py:129
  341.4 13.2 %bitcast_add_fusion = f32[16,8,128,128]{3,1,2,0:T(8,128)S(1)} fusion(f32[16,1,8,1,128,128]{5,4,3,2,1,0:T(8,128)} %param.9, f32[16,4,128,128]{3,0,2,1:T(8,128)S(1)} %fusion.14, s32[4]{0:T(128)S(1)} %and_select_fusion), kind=kOutput, calls=%fused_computation.2 | convolution fusion | flops 102760480 | bytes 20971536 | tf_op jit(solution)/shard_map/bs,asxy->abxy/dot_general | solution.py:151
  355.9 7.2 %broadcast_select_fusion = (f32[16,1,128,128]{3,1,2,0:T(1,128)}, f32[16,1,128,128]{3,1,2,0:T(1,128)S(1)}, f32[16,1,128,128]{3,1,2,0:T(1,128)S(1)}, f32[16,1,128,128]{3,1,2,0:T(1,128)S(1)}) fusion(f32[16,1,128,128]{3,1,2,0:T(1,128)} %bitcast.134, pred[]{:T(512)S(6)} %eq.267, f32[16,8,128,128]{3,1,2,0:T(8,128)S(1)} %bitcast_add_fusion, s32[]{:T(128)S(6)} %select_n.288, ...), kind=kLoop, calls=%fused_computation.23 | loop fusion | flops 262144 | bytes 9437201 | tf_op jit(solution)/shard_map/jit(_where)/select_n | solution.py:12
  365.8 154.9 %all-reduce.9.cloned.1.call-done = (f32[16,128,128]{2,1,0:T(8,128)}, f32[16,128,128]{2,1,0:T(8,128)}, f32[16,128,128]{2,1,0:T(8,128)}, f32[16,128,128]{2,1,0:T(8,128)}) async-done(((f32[16,128,128]{2,1,0:T(8,128)}, f32[16,128,128]{2,1,0:T(8,128)}, f32[16,128,128]{2,1,0:T(8,128)}, f32[16,128,128]{2,1,0:T(8,128)}), (f32[16,128,128]{2,1,0:T(8,128)}, f32[16,128,128]{2,1,0:T(8,128)}, f32[16,128,128]{2,1,0:T(8,128)}, ...) | async-done | bytes 4194320 | tf_op jit(solution)/shard_map/psum | solution.py:12
  527.6 10.3 %fusion.26 = f32[16,128,512]{2,1,0:T(8,128)} fusion(f32[16,128,512]{2,1,0:T(8,128)} %copy-done.2, f32[512,512]{1,0:T(8,128)S(1)} %copy-done), kind=kOutput, calls=%fused_computation.26 | convolution fusion | flops 6442450944 | bytes 9437184 | tf_op jit(solution)/shard_map/axp,pq->axq/dot_general | solution.py:163
  537.9 40.1 %all-reduce.7.cloned.1.call-done = f32[8,128,512]{2,1,0:T(8,128)} async-done(((f32[8,128,512]{2,1,0:T(8,128)}), f32[8,128,512]{2,1,0:T(8,128)}) %all-reduce.7.cloned.1.call-update) | async-done | bytes 2097168 | tf_op jit(solution)/shard_map/psum | solution.py:12
  578.0 18.0 %fusion.1 = f32[8,128,16,128]{3,1,2,0:T(8,128)} fusion(f32[16,128,512]{2,1,0:T(8,128)} %fusion.26, f32[8,128,512]{2,1,0:T(8,128)} %all-reduce.7.cloned.1.call-done), kind=kOutput, calls=%fused_computation.3 | convolution fusion | flops 12884901888 | bytes 14680064 | tf_op jit(solution)/shard_map/axq,byq->abxy/dot_general | solution.py:170
  596.0 9.4 %copy.60 = f32[8,128,16,128]{1,0,3,2:T(8,128)} copy(f32[8,128,16,128]{3,1,2,0:T(8,128)} %fusion.1) | data formatting | bytes 16777216 | tf_op jit(solution)/shard_map/axq,byq->abxy/dot_general | solution.py:170
  605.4 10.1 %fusion = f32[16,1,8,1,128,128]{5,2,4,0,3,1:T(8,128)} fusion(f32[16,8,128,128]{3,1,2,0:T(8,128)} %copy-done.1, f32[8,128,16,128]{1,0,3,2:T(8,128)} %copy.60, pred[16,8]{1,0:T(8,128)(4,1)S(1)} %compare_and_fusion), kind=kLoop, calls=%fused_computation.1 | loop fusion | flops 4194304 | bytes 25165952 | tf_op jit(solution)/shard_map/broadcast_in_dim | solution.py:177
  615.6 8.2 %copy.61 = f32[16,1,8,1,128,128]{5,4,3,2,1,0:T(8,128)} copy(f32[16,1,8,1,128,128]{5,2,4,0,3,1:T(8,128)} %fusion) | data formatting | bytes 16777216 | tf_op jit(solution)/shard_map/broadcast_in_dim | solution.py:177
  (68 shorter events, 30.0 us)
Async XLA Ops:
  6.5 521.1 %copy-start = (f32[512,512]{1,0:T(8,128)S(1)}, f32[512,512]{1,0:T(8,128)}, u32[]{:S(2)}) copy-start(f32[512,512]{1,0:T(8,128)} %param.15) | copy-start | bytes 3145732
  6.5 27.7 %all-gather.2.cloned.1.call-start = ((), (), s32[]{:S(2)}) async-start(), calls=%async_computation.4 | async-start | bytes 2621440 | tf_op jit(solution)/shard_map/all_gather | solution.py:61
  7.3 142.8 %reduce-scatter.2.cloned.1.call-start = ((), (), s32[]{:S(2)}) async-start(), calls=%async_computation.5 | async-start | bytes 4718592 | tf_op jit(solution)/shard_map/reduce_scatter | solution.py:71
  61.6 0.9 copy-start.5
  61.6 1.7 copy-start.6
  61.6 4.2 copy-start.7
  61.6 122.2 %all-reduce.5.cloned.1.call-start = ((), (), s32[]{:S(2)}) async-start(), calls=%async_computation.3 | async-start | bytes 262144 | tf_op jit(solution)/shard_map/psum | solution.py:12
  194.5 29.4 %all-to-all-start = ((f32[4,2,4,128,128]{4,1,3,2,0:T(2,128)}), f32[4,2,4,128,128]{4,1,3,2,0:T(2,128)S(1)}, u32[]{:S(2)}, u32[]{:S(2)}) async-start(f32[4,2,4,128,128]{4,1,3,2,0:T(2,128)} %fusion.11), calls=%async_computation.1 | async-start | bytes 4194304 | tf_op jit(solution)/shard_map/all_to_all | solution.py:108
  233.6 98.5 %all-to-all-start.1 = ((f32[8,8,128,128]{3,2,1,0:T(8,128)}), f32[8,8,128,128]{3,2,1,0:T(8,128)}, u32[]{:S(2)}, u32[]{:S(2)}) async-start(f32[8,8,128,128]{3,2,1,0:T(8,128)} %copy.51), calls=%async_computation.2 | async-start | bytes 8388608 | tf_op jit(solution)/shard_map/all_to_all | solution.py:126
  239.1 281.7 %all-reduce.9.cloned.1.call-start = ((), (), s32[]{:S(2)}) async-start(), calls=%async_computation.7 | async-start | bytes 8388608 | tf_op jit(solution)/shard_map/psum | solution.py:12
  354.6 8.5 %copy-start.1 = (f32[16,8,128,128]{3,1,2,0:T(8,128)}, f32[16,8,128,128]{3,1,2,0:T(8,128)S(1)}, u32[]{:S(2)}) copy-start(f32[16,8,128,128]{3,1,2,0:T(8,128)S(1)} %bitcast_add_fusion) | copy-start | bytes 25165828
  365.8 212.2 %all-reduce.7.cloned.1.call-start = ((), (), s32[]{:S(2)}) async-start(), calls=%async_computation.6 | async-start | bytes 4194304 | tf_op jit(solution)/shard_map/psum | solution.py:12
  520.8 2.9 copy-start.4
  520.8 3.0 copy-start.3
  523.9 2.0 copy-start.2
Sparse Core Ops, SparseCore 0:
  8.9 25.2 all-gather.1
  61.7 88.3 reduce-scatter.1
  152.4 31.3 all-reduce.4
  365.9 154.7 all-reduce.8
  527.6 50.3 all-reduce.6
where the time goes:
time: 635 us; the launch traced here: 631 us
  waiting for transfers between devices  451 us (71%)
  matrix products  80.7 us (13%)
  local copies, waits for them, and re-layouts  50.6 us (8%)
  other arithmetic  23.6 us (4%)
  between operations  14.4 us (2%)
  starting transfers between devices  10.3 us (2%)
    psum x3, waiting for transfers between devices, spread_2(): return lax.psum(jnp.where(mine, x, jnp.zeros_like(x)), axis)  222 us
    all_to_all x1, waiting for transfers between devices, per_device(): lax.all_to_all(packed, 'col', split_axis=0, concat_axis=0, tiled=True)  91.6 us
    reduce_scatter x1, waiting for transfers between devices, per_device(): lax.psum_scatter(products.reshape(lax.axis_size('col') * local_cols, loca...  83.9 us
    all_gather x1, waiting for transfers between devices, per_device(): all_pivots = lax.all_gather(pivot_basis, 'row', axis=1, tiled=True)  26.9 us
    all_to_all x1, waiting for transfers between devices, per_device(): lax.all_to_all(packed, 'row', split_axis=0, concat_axis=0, tiled=True)  25.6 us
    dot_general x1, matrix products, per_device(): jnp.einsum('axq,byq->abxy', scaled, col_panel, precision=highest, preferr...  18 us
    dot_general x1, matrix products, per_device(): jnp.einsum('bs,asxy->abxy', col_place, spread, precision=highest, preferr...  13.2 us
  transfers between devices with their start and end apart: 7, of which 7 were waited for; matrix products, arithmetic and copies ran while one was open for 3% of the time, Pallas kernels for 0%

commit v1 on v0

--- a/solution.py
+++ b/solution.py
@@ -9,7 +9,7 @@
 
 def spread_2(x, axis, root):
     mine = lax.axis_index(axis) == root
-    return lax.psum(jnp.where(mine, x, jnp.zeros_like(x)), axis)
+    return jnp.sum(lax.all_gather(jnp.where(mine, x, jnp.zeros_like(x)), axis), axis=0)
 
 
 def select_entries(lookup, wanted):

time: 635 us -> 952 us (1.50)
  waiting for transfers between devices: 451 us -> 751 us
  other arithmetic: 23.6 us -> 44.3 us
    all_gather x0 -> x5, waiting for transfers between devices: none -> 528 us  [spread_2(): lax.all_gather(jnp.where(mine, x, jnp.zeros_like(x)), axis)]
    psum x3 -> x0, waiting for transfers between devices: 222 us -> none  [spread_2(): return lax.psum(jnp.where(mine, x, jnp.zeros_like(x)), axis)]
    reduce_sum x0 -> x6, other arithmetic: none -> 22.6 us  [spread_2(): jnp.sum(lax.all_gather(jnp.where(mine, x, jnp.zeros_like(x)), axis), axis=0)]
  transfers between devices with their start and end apart: 7 -> 9, of which waited for: 7 -> 9; matrix products, arithmetic and copies ran while one was open for 3% -> 3% of each run, Pallas kernels for 0% -> 0%
where the time goes in v1:
time: 952 us; the launch traced here: 947 us
  waiting for transfers between devices  751 us (79%)
  matrix products  75.8 us (8%)
  local copies, waits for them, and re-layouts  44.8 us (5%)
  other arithmetic  44.3 us (5%)
  between operations  14.9 us (2%)
    all_gather x5, waiting for transfers between devices, spread_2(): lax.all_gather(jnp.where(mine, x, jnp.zeros_like(x)), axis)  528 us
    all_to_all x1, waiting for transfers between devices, per_device(): lax.all_to_all(packed, 'col', split_axis=0, concat_axis=0, tiled=True)  91.7 us
    reduce_scatter x1, waiting for transfers between devices, per_device(): lax.psum_scatter(products.reshape(lax.axis_size('col') * local_cols, loca...  75.9 us
    all_gather x1, waiting for transfers between devices, per_device(): all_pivots = lax.all_gather(pivot_basis, 'row', axis=1, tiled=True)  26.9 us
    all_to_all x1, waiting for transfers between devices, per_device(): lax.all_to_all(packed, 'row', split_axis=0, concat_axis=0, tiled=True)  25.6 us
    reduce_sum x6, other arithmetic, spread_2(): jnp.sum(lax.all_gather(jnp.where(mine, x, jnp.zeros_like(x)), axis), axis=0)  22.6 us
  transfers between devices with their start and end apart: 9, of which 9 were waited for; matrix products, arithmetic and copies ran while one was open for 3% of the time, Pallas kernels for 0%

profile of v1, /device:TPU:0, one launch (start us, length us, event | category | flops | bytes accessed | tf_op | source)
XLA Modules:
  0.0 947.0 jit_solution(3371567236761242922)
XLA Ops:
  7.3 26.9 %all-gather.13.cloned.1.call-done = f32[8,4,64,256]{3,2,1,0:T(8,128)} async-done(((f32[8,1,64,256]{3,2,1,0:T(8,128)}), f32[8,4,64,256]{3,2,1,0:T(8,128)}) %all-gather.13.cloned.1.call-update) | async-done | bytes 2097168 | tf_op jit(solution)/shard_map/all_gather | solution.py:61
  34.2 10.3 %convolution_bitcast_fusion = f32[8,4,8,64,64]{3,4,2,0,1:T(8,128)} fusion(f32[4,8,64,256,1]{3,2,4,1,0:T(8,128)} %bitcast.133, f32[8,1,64,256]{3,2,1,0:T(8,128)} %param.11), kind=kOutput, calls=%fused_computation.15 | convolution fusion | flops 3221225472 | bytes 6815744 | tf_op jit(solution)/shard_map/trp,scup->cstru/dot_general | solution.py:64
  44.5 9.2 copy.50
  53.7 7.9 reshape.541
  64.9 7.3 all-gather
  74.2 75.9 %reduce-scatter.2.cloned.1.call-done = f32[4,8,4096]{2,1,0:T(8,128)} async-done(((f32[32,8,4096]{2,1,0:T(8,128)}), f32[4,8,4096]{2,1,0:T(8,128)}) %reduce-scatter.2.cloned.1.call-update) | async-done | bytes 524304 | tf_op jit(solution)/shard_map/reduce_scatter | solution.py:71
  169.1 25.6 %all-to-all-done = f32[4,2,4,128,128]{4,1,3,2,0:T(2,128)S(1)} async-done(((f32[4,2,4,128,128]{4,1,3,2,0:T(2,128)}), f32[4,2,4,128,128]{4,1,3,2,0:T(2,128)S(1)}, u32[]{:S(2)}, u32[]{:S(2)}) %all-to-all-start) | async-done | bytes 2097184 | tf_op jit(solution)/shard_map/all_to_all | solution.py:108
  204.4 4.7 all-to-all-start.1
  210.6 91.7 %all-to-all-done.1 = f32[8,8,128,128]{3,2,1,0:T(8,128)} async-done(((f32[8,8,128,128]{3,2,1,0:T(8,128)}), f32[8,8,128,128]{3,2,1,0:T(8,128)}, u32[]{:S(2)}, u32[]{:S(2)}) %all-to-all-start.1) | async-done | bytes 4194336 | tf_op jit(solution)/shard_map/all_to_all | solution.py:126
  302.3 6.4 fusion.22
  311.5 13.5 %bitcast_add_fusion = f32[16,8,128,128]{3,1,2,0:T(8,128)S(1)} fusion(f32[16,1,8,1,128,128]{5,4,3,2,1,0:T(8,128)} %param.9, f32[16,4,128,128]{3,0,2,1:T(8,128)S(1)} %fusion.13, s32[4]{0:T(128)S(1)} %and_select_fusion), kind=kOutput, calls=%fused_computation.7 | convolution fusion | flops 102760480 | bytes 20971536 | tf_op jit(solution)/shard_map/bs,asxy->abxy/dot_general | solution.py:151
  325.0 5.9 broadcast_select_fusion.3
  332.7 121.1 %all-gather.21.cloned.1.call-done = f32[128,1,128,128]{3,2,1,0:T(8,128)} async-done(((f32[16,1,128,128]{3,2,1,0:T(8,128)}), f32[128,1,128,128]{3,2,1,0:T(8,128)}) %all-gather.21.cloned.1.call-update) | async-done | bytes 8388624 | tf_op jit(solution)/shard_map/all_gather | solution.py:12
  458.0 120.5 %all-gather.19.cloned.1.call-done = f32[128,1,128,128]{3,2,1,0:T(8,128)} async-done(((f32[16,1,128,128]{3,2,1,0:T(8,128)}), f32[128,1,128,128]{3,2,1,0:T(8,128)}) %all-gather.19.cloned.1.call-update) | async-done | bytes 8388624 | tf_op jit(solution)/shard_map/all_gather | solution.py:12
  582.7 120.5 %all-gather.17.cloned.1.call-done = f32[128,1,128,128]{3,2,1,0:T(8,128)} async-done(((f32[16,1,128,128]{3,2,1,0:T(8,128)}), f32[128,1,128,128]{3,2,1,0:T(8,128)}) %all-gather.17.cloned.1.call-update) | async-done | bytes 8388624 | tf_op jit(solution)/shard_map/all_gather | solution.py:12
  703.2 5.1 bitcast_reduce_fusion.3
  708.3 119.5 %all-gather.15.cloned.1.call-done = f32[128,1,128,128]{3,2,1,0:T(8,128)} async-done(((f32[16,1,128,128]{3,2,1,0:T(8,128)}), f32[128,1,128,128]{3,2,1,0:T(8,128)}) %all-gather.15.cloned.1.call-update) | async-done | bytes 8388624 | tf_op jit(solution)/shard_map/all_gather | solution.py:12
  835.0 9.7 %fusion.25 = f32[16,128,512]{2,1,0:T(8,128)} fusion(f32[512,512]{1,0:T(8,128)S(1)} %copy-done, f32[16,128,128]{2,1,0:T(8,128)S(1)} %bitcast_reduce_fusion.1, f32[16,128,128]{2,1,0:T(8,128)S(1)} %bitcast_reduce_fusion.2, f32[16,128,128]{2,1,0:T(8,128)} %bitcast_reduce_fusion.3, f32[16,128,128]{2,1,0:T(8,128)} %copy-done.4), kind=kOutput, calls=%fused_computation.34 | convolution fusion | flops 6445596672 | bytes 9437184 | tf_op jit(solution)/shard_map/axp,pq->axq/dot_general | solution.py:163
  844.7 46.8 %all-gather.23.cloned.1.call-done = f32[32,1,128,512]{3,2,1,0:T(8,128)} async-done(((f32[8,1,128,512]{3,2,1,0:T(8,128)}), f32[32,1,128,512]{3,2,1,0:T(8,128)}) %all-gather.23.cloned.1.call-update) | async-done | bytes 8388624 | tf_op jit(solution)/shard_map/all_gather | solution.py:12
  891.5 4.8 bitcast_reduce_fusion
  896.3 15.8 %fusion.1 = f32[8,128,16,128]{3,1,2,0:T(8,128)} fusion(f32[16,128,512]{2,1,0:T(8,128)S(1)} %copy-done.2, f32[8,128,512]{2,1,0:T(8,128)S(1)} %bitcast_reduce_fusion), kind=kOutput, calls=%fused_computation.9 | convolution fusion | flops 12884901888 | bytes 14680064 | tf_op jit(solution)/shard_map/axq,byq->abxy/dot_general | solution.py:170
  912.1 9.4 copy.63
  921.5 10.2 %fusion = f32[16,1,8,1,128,128]{5,2,4,0,3,1:T(8,128)} fusion(f32[16,8,128,128]{3,1,2,0:T(8,128)} %copy-done.1, f32[8,128,16,128]{1,0,3,2:T(8,128)} %copy.63, pred[16,8]{1,0:T(8,128)(4,1)S(1)} %compare_and_fusion), kind=kLoop, calls=%fused_computation.1 | loop fusion | flops 4194304 | bytes 25165952 | tf_op jit(solution)/shard_map/broadcast_in_dim | solution.py:177
  931.7 8.2 copy.64
  (93 shorter events, 55.3 us)
Async XLA Ops:
  6.5 828.4 %copy-start = (f32[512,512]{1,0:T(8,128)S(1)}, f32[512,512]{1,0:T(8,128)}, u32[]{:S(2)}) copy-start(f32[512,512]{1,0:T(8,128)} %param.15) | copy-start | bytes 3145732
  6.5 27.7 %all-gather.13.cloned.1.call-start = ((), (), s32[]{:S(2)}) async-start(), calls=%async_computation.3 | async-start | bytes 2621440 | tf_op jit(solution)/shard_map/all_gather | solution.py:61
  7.3 142.9 %reduce-scatter.2.cloned.1.call-start = ((), (), s32[]{:S(2)}) async-start(), calls=%async_computation.4 | async-start | bytes 4718592 | tf_op jit(solution)/shard_map/reduce_scatter | solution.py:71
  61.6 3.0 copy-start.12
  61.6 3.4 copy-start.5
  64.5 9.0 copy-start.15
  155.7 5.4 copy-start.7
  155.7 5.4 copy-start.8
  161.1 8.0 copy-start.16
  161.1 8.0 copy-start.10
  165.1 32.8 %copy-start.6 = (s32[4]{0:T(128)S(1)}, s32[4]{0:T(128)}, u32[]{:S(2)}) copy-start(s32[4]{0:T(128)} %get-tuple-element.14) | copy-start | bytes 52
  165.1 29.6 %all-to-all-start = ((f32[4,2,4,128,128]{4,1,3,2,0:T(2,128)}), f32[4,2,4,128,128]{4,1,3,2,0:T(2,128)S(1)}, u32[]{:S(2)}, u32[]{:S(2)}) async-start(f32[4,2,4,128,128]{4,1,3,2,0:T(2,128)} %fusion.10), calls=%async_computation.1 | async-start | bytes 4194304 | tf_op jit(solution)/shard_map/all_to_all | solution.py:108
  204.4 5.8 copy-start.9
  204.4 5.8 copy-start.14
  204.4 6.0 copy-start.11
  204.4 97.9 %all-to-all-start.1 = ((f32[8,8,128,128]{3,2,1,0:T(8,128)}), f32[8,8,128,128]{3,2,1,0:T(8,128)}, u32[]{:S(2)}, u32[]{:S(2)}) async-start(f32[8,8,128,128]{3,2,1,0:T(8,128)} %copy.55), calls=%async_computation.2 | async-start | bytes 8388608 | tf_op jit(solution)/shard_map/all_to_all | solution.py:126
  209.1 244.7 %all-gather.21.cloned.1.call-start = ((), (), s32[]{:S(2)}) async-start(), calls=%async_computation.8 | async-start | bytes 9437184 | tf_op jit(solution)/shard_map/all_gather | solution.py:12
  325.0 5.9 copy-start.1
  330.9 247.6 %all-gather.19.cloned.1.call-start = ((), (), s32[]{:S(2)}) async-start(), calls=%async_computation.7 | async-start | bytes 9437184 | tf_op jit(solution)/shard_map/all_gather | solution.py:12
  331.5 371.7 %all-gather.17.cloned.1.call-start = ((), (), s32[]{:S(2)}) async-start(), calls=%async_computation.6 | async-start | bytes 9437184 | tf_op jit(solution)/shard_map/all_gather | solution.py:12
  332.1 495.7 %all-gather.15.cloned.1.call-start = ((), (), s32[]{:S(2)}) async-start(), calls=%async_computation.5 | async-start | bytes 9437184 | tf_op jit(solution)/shard_map/all_gather | solution.py:12
  332.7 558.8 %all-gather.23.cloned.1.call-start = ((), (), s32[]{:S(2)}) async-start(), calls=%async_computation.9 | async-start | bytes 10485760 | tf_op jit(solution)/shard_map/all_gather | solution.py:12
  827.8 4.3 copy-start.3
  891.5 4.8 copy-start.2
  (2 other events, 3.0 us)
Sparse Core Ops, SparseCore 0:
  8.9 25.2 all-gather.12
  61.7 88.3 reduce-scatter.1
  331.0 122.7 all-gather.20
  455.8 122.6 all-gather.18
  580.5 122.6 all-gather.16
  705.1 122.6 all-gather.14
  835.0 56.4 all-gather.22
